TPU v7x, 32 devices: a whole 2x2x4 slice. The times are simulated.
32 devices in a mesh: ctx: 8 (over z, y), wt: 4 (over x, core).
Axes of the slice: x: 2, y: 2, z: 4, core: 2. Of those that a mesh axis runs over, the one named last changes fastest.
Arguments:
- layer_input: bfloat16 [4, 1024, 1024], P('wt', 'ctx'), may hold values from -6 to 6
- out_grad: bfloat16 [4, 1024, 1024], P('wt', 'ctx'), may hold values from -6 to 6
- deal: int32 [8, 2], replicated, may hold values from 0 to 15, as said below
- w_qkv: bfloat16 [1024, 3072], P('wt'), may hold values from -0.1875 to 0.1875
- w_out: bfloat16 [1024, 1024], P('wt'), may hold values from -0.1875 to 0.1875
- w_up: bfloat16 [1024, 4096], P('wt'), may hold values from -0.1875 to 0.1875
- w_down: bfloat16 [4096, 1024], P('wt'), may hold values from -0.09375 to 0.09375
- norm_gain: bfloat16 [4, 1024], P(None, 'wt'), may hold values from 0.099609375 to 1.8984375
- norm_shift: bfloat16 [4, 1024], P(None, 'wt'), may hold values from -1.5 to 1.5
- bias_width: bfloat16 [4, 1024], P(None, 'wt'), may hold values from -2.5 to 2.5
- up_bias: bfloat16 [4096], P('wt'), may hold values from -2.5 to 2.5
Outputs:
- layer_out: bfloat16 [4, 1024, 1024], P('wt', 'ctx')
- input_grad: float32 [4, 1024, 1024], P('wt', 'ctx')
- grad_qkv: float32 [1024, 3072], P('wt')
- grad_out: float32 [1024, 1024], P('wt')
- grad_up: float32 [1024, 4096], P('wt')
- grad_down: float32 [4096, 1024], P('wt')
- grad_gain: float32 [4, 1024], P(None, 'wt')
- grad_shift: float32 [4, 1024], P(None, 'wt')
- grad_bias: float32 [4, 1024], P(None, 'wt')
- grad_up_bias: float32 [4096], P('wt')
Inputs may be any that keep to these rules, and one draw needn't show every extreme that they name: `deal`: pieces of 64 tokens are numbered along a sequence. Row j holds a number p below 8 and its mirror 1024 // 64 - 1 - p; every piece appears once.
All inputs are finite; a program needn't handle non-finite values.
Results may differ from a plain program's by a relative error of at most 0.015.
Values may be sent and summed in bfloat16 or wider, within the bound.
No kernel may reach another device: no remote copies, remote signals or barrier semaphores. Data moves between devices by JAX's collectives and lax.ppermute only.
A program may use at most 320 MiB of HBM per device.

v0:
```python
import math
import jax
import jax.numpy as jnp
from jax import lax
from jax.sharding import PartitionSpec as P

HEADS = 16
BLK = 256
PIECE = 64
epsilon = 1e-05
relax = 32.0


def layer_norm(value, gain, shift):
    mean = jnp.mean(value, axis=-1, keepdims=True)
    centered = value - mean
    spread = jnp.mean(centered * centered, axis=-1, keepdims=True)
    return centered * lax.rsqrt(spread + epsilon) * gain + shift


def gelu_tanh(value):
    return jax.nn.gelu(value, approximate=True)


def rows_dot(left, weight):
    return jnp.einsum("std,de->ste", left, weight, preferred_element_type=jnp.float32)


def weight_grad(left, right):
    return jnp.einsum("std,ste->de", left, right, preferred_element_type=jnp.float32)


def back_dot(grad, weight):
    return jnp.einsum("ste,de->std", grad, weight, preferred_element_type=jnp.float32)


def row_total(value):
    return jnp.sum(value.astype(jnp.float32), axis=(0, 1))


def per_device(
    layer_input,
    out_grad,
    deal,
    w_qkv,
    w_out,
    w_up,
    w_down,
    norm_gain,
    norm_shift,
    bias_width,
    up_bias,
):
    seqs, rows, width = layer_input.shape
    heads = HEADS
    head = width // heads
    prescale = 1.0 / (relax * math.sqrt(head))
    ranks = lax.axis_size("ctx")
    length = rows * ranks
    per_block = BLK // PIECE
    rank = lax.axis_index("ctx")
    chosen = jnp.arange(ranks, dtype=jnp.int32) == rank
    mine = jnp.sum(jnp.where(chosen[:, None], deal, 0), axis=0)
    query_blocks = jnp.repeat(mine, rows // 2) // per_block
    key_blocks = jnp.repeat(deal.reshape(-1), rows // 2) // per_block
    full_qkv, full_out, full_up, full_down, gains, shifts, biases, up_shift = (
        lax.all_gather(w_qkv, "wt", axis=0, tiled=True),
        lax.all_gather(w_out, "wt", axis=0, tiled=True),
        lax.all_gather(w_up, "wt", axis=0, tiled=True),
        lax.all_gather(w_down, "wt", axis=0, tiled=True),
        lax.all_gather(norm_gain, "wt", axis=1, tiled=True),
        lax.all_gather(norm_shift, "wt", axis=1, tiled=True),
        lax.all_gather(bias_width, "wt", axis=1, tiled=True),
        lax.all_gather(up_bias, "wt", axis=0, tiled=True),
    )
    gains = gains.astype(jnp.float32)
    shifts = shifts.astype(jnp.float32)
    biases = biases.astype(jnp.float32)
    up_shift = up_shift.astype(jnp.float32)
    input_float = layer_input.astype(jnp.float32)
    first = layer_norm(input_float, gains[0], shifts[0]).astype(jnp.bfloat16)
    mixed = rows_dot(first, full_qkv)
    query = (mixed[..., :width] + biases[0]).astype(jnp.bfloat16)
    kv_local = jnp.concatenate(
        [mixed[..., width : 2 * width], mixed[..., 2 * width :] + biases[1]], axis=-1
    ).astype(jnp.bfloat16)
    kv_all = lax.all_gather(kv_local, "ctx", axis=1, tiled=True)
    step = math.gcd(length, 1024)
    count = length // step
    query4 = query.reshape(seqs, rows, heads, head)

    def score_block(left, right):
        return (
            jnp.einsum("sqhd,skhd->shqk", left, right, preferred_element_type=jnp.float32)
            * prescale
        )

    def key_block(index):
        start = index * step
        piece = lax.dynamic_slice_in_dim(kv_all, start, step, 1)
        keys4 = piece[..., :width].reshape(seqs, step, heads, head)
        values4 = piece[..., width:].reshape(seqs, step, heads, head)
        visible = (
            query_blocks[:, None] >= lax.dynamic_slice_in_dim(key_blocks, start, step, 0)[None, :]
        )
        return (keys4, values4, visible)

    def probs(raw, visible, totals):
        return jnp.where(visible, jnp.exp(raw * relax - totals[..., None]), 0.0)

    def online(index, carry):
        top, total, acc = carry
        keys4, values4, visible = key_block(index)
        raw = jnp.where(visible, score_block(query4, keys4), -1e30)
        new_top = jnp.maximum(top, jnp.max(raw, axis=-1))
        terms = jnp.where(visible, jnp.exp((raw - new_top[..., None]) * relax), 0.0)
        factor = jnp.exp((top - new_top) * relax)
        total = total * factor + jnp.sum(terms, axis=-1)
        acc = acc * jnp.transpose(factor, (0, 2, 1))[..., None]
        acc = acc + jnp.einsum(
            "shqk,skhd->sqhd",
            terms.astype(jnp.bfloat16),
            values4,
            preferred_element_type=jnp.float32,
        )
        return (new_top, total, acc)

    start_top = jnp.full((seqs, heads, rows), -1e30, jnp.float32)
    start_total = jnp.zeros((seqs, heads, rows), jnp.float32)
    start_acc = jnp.zeros((seqs, rows, heads, head), jnp.float32)
    top, total, acc = lax.fori_loop(0, count, online, (start_top, start_total, start_acc))
    log_total = top * relax + jnp.log(total)
    attended_float = acc / jnp.transpose(total, (0, 2, 1))[..., None]
    attended = attended_float.reshape(seqs, rows, width).astype(jnp.bfloat16)
    branch = rows_dot(attended, full_out) + biases[2]
    resid = input_float + layer_norm(branch, gains[1], shifts[1])
    second = layer_norm(resid, gains[2], shifts[2]).astype(jnp.bfloat16)
    upper = rows_dot(second, full_up) + up_shift
    hidden = gelu_tanh(upper).astype(jnp.bfloat16)
    ffn = rows_dot(hidden, full_down) + biases[3]
    top_norm, pull_four = jax.vjp(layer_norm, ffn, gains[3], shifts[3])
    result = resid + top_norm
    d_out = out_grad.astype(jnp.float32)
    d_ffn, d_gain3, d_shift3 = pull_four(d_out)
    d_ffn = d_ffn.astype(jnp.bfloat16)
    d_bias3 = row_total(d_ffn)
    g_down = weight_grad(hidden, d_ffn)
    d_hidden = back_dot(d_ffn, full_down)
    _, pull_gelu = jax.vjp(gelu_tanh, upper)
    d_upper = pull_gelu(d_hidden)[0].astype(jnp.bfloat16)
    d_up_shift = row_total(d_upper)
    g_up = weight_grad(second, d_upper)
    d_second = back_dot(d_upper, full_up)
    _, pull_three = jax.vjp(layer_norm, resid, gains[2], shifts[2])
    d_resid_part, d_gain2, d_shift2 = pull_three(d_second)
    d_resid = d_out + d_resid_part
    _, pull_two = jax.vjp(layer_norm, branch, gains[1], shifts[1])
    d_branch, d_gain1, d_shift1 = pull_two(d_resid)
    d_branch = d_branch.astype(jnp.bfloat16)
    d_bias2 = row_total(d_branch)
    g_out = weight_grad(attended, d_branch)
    d_attended = back_dot(d_branch, full_out).astype(jnp.bfloat16)
    d_out4 = d_attended.reshape(seqs, rows, heads, head)
    delta = jnp.einsum("sqhd,sqhd->shq", d_out4.astype(jnp.float32), attended_float)

    def score_grads(q_rows, do_rows, k_rows, v_rows, visible, lse_rows, delta_rows):
        weights = probs(score_block(q_rows, k_rows), visible, lse_rows)
        d_probs = jnp.einsum("sqhd,skhd->shqk", do_rows, v_rows, preferred_element_type=jnp.float32)
        d_scores = (relax * weights * (d_probs - delta_rows[..., None])).astype(jnp.bfloat16)
        return (d_scores, weights.astype(jnp.bfloat16))

    zero_query = jnp.zeros((seqs, rows, heads, head), jnp.float32)

    def local_grads(d_query, index):
        keys4, values4, visible = key_block(index)
        d_scores, weights = score_grads(query4, d_out4, keys4, values4, visible, log_total, delta)
        d_query = (
            d_query
            + jnp.einsum("shqk,skhd->sqhd", d_scores, keys4, preferred_element_type=jnp.float32)
            * prescale
        )
        d_keys = (
            jnp.einsum("shqk,sqhd->kshd", d_scores, query4, preferred_element_type=jnp.float32)
            * prescale
        )
        d_values = jnp.einsum(
            "shqk,sqhd->kshd", weights, d_out4, preferred_element_type=jnp.float32
        )
        joined = jnp.concatenate(
            [d_keys.reshape(step, seqs, width), d_values.reshape(step, seqs, width)], axis=-1
        )
        return (d_query, joined)

    d_query, pieces = lax.scan(local_grads, zero_query, jnp.arange(count, dtype=jnp.int32))
    terms = pieces.reshape(length, seqs, 2 * width)
    d_kv = jnp.transpose(lax.psum_scatter(terms, "ctx", scatter_dimension=0, tiled=True), (1, 0, 2))
    d_query = d_query.reshape(seqs, rows, width).astype(jnp.bfloat16)
    d_kv = d_kv.astype(jnp.bfloat16)
    d_bias0 = row_total(d_query)
    d_bias1 = row_total(d_kv[..., width:])
    d_mixed = jnp.concatenate([d_query, d_kv], axis=-1)
    g_qkv = weight_grad(first, d_mixed)
    d_first = back_dot(d_mixed, full_qkv)
    _, pull_one = jax.vjp(layer_norm, input_float, gains[0], shifts[0])
    d_input_part, d_gain0, d_shift0 = pull_one(d_first)
    input_grad = d_resid + d_input_part
    grad_gain = jnp.stack([d_gain0, d_gain1, d_gain2, d_gain3])
    grad_shift = jnp.stack([d_shift0, d_shift1, d_shift2, d_shift3])
    grad_bias = jnp.stack([d_bias0, d_bias1, d_bias2, d_bias3])
    owned = (
        lax.psum_scatter(g_qkv.astype(jnp.bfloat16), "wt", scatter_dimension=0, tiled=True).astype(
            jnp.float32
        ),
        lax.psum_scatter(g_out.astype(jnp.bfloat16), "wt", scatter_dimension=0, tiled=True).astype(
            jnp.float32
        ),
        lax.psum_scatter(g_up.astype(jnp.bfloat16), "wt", scatter_dimension=0, tiled=True).astype(
            jnp.float32
        ),
        lax.psum_scatter(g_down.astype(jnp.bfloat16), "wt", scatter_dimension=0, tiled=True).astype(
            jnp.float32
        ),
        lax.psum_scatter(
            grad_gain.astype(jnp.bfloat16), "wt", scatter_dimension=1, tiled=True
        ).astype(jnp.float32),
        lax.psum_scatter(
            grad_shift.astype(jnp.bfloat16), "wt", scatter_dimension=1, tiled=True
        ).astype(jnp.float32),
        lax.psum_scatter(
            grad_bias.astype(jnp.bfloat16), "wt", scatter_dimension=1, tiled=True
        ).astype(jnp.float32),
        lax.psum_scatter(
            d_up_shift.astype(jnp.bfloat16), "wt", scatter_dimension=0, tiled=True
        ).astype(jnp.float32),
    )
    summed = lax.psum(
        (owned[0], owned[1], owned[2], owned[3], owned[4], owned[5], owned[6], owned[7]), "ctx"
    )
    return (
        result.astype(jnp.bfloat16),
        input_grad,
        summed[0],
        summed[1],
        summed[2],
        summed[3],
        summed[4],
        summed[5],
        summed[6],
        summed[7],
    )


def solution(mesh):
    in_specs = (
        P("wt", "ctx", None),
        P("wt", "ctx", None),
        P(),
        P("wt", None),
        P("wt", None),
        P("wt", None),
        P("wt", None),
        P(None, "wt"),
        P(None, "wt"),
        P(None, "wt"),
        P("wt"),
    )
    out_specs = (
        P("wt", "ctx", None),
        P("wt", "ctx", None),
        P("wt", None),
        P("wt", None),
        P("wt", None),
        P("wt", None),
        P(None, "wt"),
        P(None, "wt"),
        P(None, "wt"),
        P("wt"),
    )
    return jax.shard_map(
        per_device, mesh=mesh, in_specs=in_specs, out_specs=out_specs, check_vma=False
    )
```

profile of v0, /device:TPU:0, one launch (start us, length us, event | category | flops | bytes accessed | tf_op | source)
XLA Modules:
  0.0 1275.9 jit_solution(7949901151484038611)
XLA Ops:
  8.0 6.3 all_gather.30
  14.2 5.5 all_gather.28
  19.7 5.3 all_gather.27
  29.1 29.6 %all-gather.6.cloned.1.call-done = bf16[1024,3072]{1,0:T(8,128)(2,1)} async-done(((bf16[256,3072]{1,0:T(8,128)(2,1)}), bf16[1024,3072]{1,0:T(8,128)(2,1)}) %all-gather.6.cloned.1.call-update) | async-done | bytes 6291472 | tf_op jit(solution)/shard_map/all_gather | solution.py:67
  58.7 4.0 convolution_bitcast_fusion
  65.7 5.2 all_gather.34
  72.4 64.9 %all-gather.8.cloned.1.call-done = bf16[1,1024,2048]{2,1,0:T(8,128)(2,1)} async-done(((bf16[1,128,2048]{2,1,0:T(8,128)(2,1)}), bf16[1,1024,2048]{2,1,0:T(8,128)(2,1)}) %all-gather.8.cloned.1.call-update) | async-done | bytes 4194320 | tf_op jit(solution)/shard_map/all_gather | solution.py:87
  137.3 4.7 fusion.90
  145.4 3.9 copy.38
  165.5 54.0 %all-gather.12.cloned.1.call-done = bf16[1024,4096]{1,0:T(8,128)(2,1)} async-done(((bf16[256,4096]{1,0:T(8,128)(2,1)}), bf16[1024,4096]{1,0:T(8,128)(2,1)}) %all-gather.12.cloned.1.call-update) | async-done | bytes 8388624 | tf_op jit(solution)/shard_map/all_gather | solution.py:69
  219.5 6.1 convolution_add_fusion
  225.6 53.7 %all-gather.14.cloned.1.call-done = bf16[4096,1024]{1,0:T(8,128)(2,1)} async-done(((bf16[1024,1024]{1,0:T(8,128)(2,1)}), bf16[4096,1024]{1,0:T(8,128)(2,1)}) %all-gather.14.cloned.1.call-update) | async-done | bytes 8388624 | tf_op jit(solution)/shard_map/all_gather | solution.py:70
  279.2 5.8 fusion.96
  287.8 4.7 fusion.98
  302.6 4.7 fusion.4
  307.3 5.8 multiply_convert_fusion
  315.1 4.1 pad_maximum_fusion
  322.2 7.0 convolution_convert_fusion.1
  330.2 7.2 convolution_convert_fusion
  338.7 3.9 fusion.97
  342.6 126.1 %reduce-scatter.15.cloned.1.call-done = f32[128,1,2048]{0,2,1:T(8,128)} async-done(((f32[1024,1,2048]{0,2,1:T(8,128)}), f32[128,1,2048]{0,2,1:T(8,128)}) %reduce-scatter.15.cloned.1.call-update) | async-done | bytes 1048592 | tf_op jit(solution)/shard_map/reduce_scatter | solution.py:196
  470.1 5.1 fusion.43
  478.7 4.6 convolution_convert_fusion.2
  485.2 7.3 all-reduce
  492.6 10.0 reduce-scatter.19.cloned.1.call-done
  502.6 74.4 %reduce-scatter.21.cloned.1.call-done = bf16[256,4096]{1,0:T(8,128)(2,1)} async-done(((bf16[1024,4096]{1,0:T(8,128)(2,1)}), bf16[256,4096]{1,0:T(8,128)(2,1)}) %reduce-scatter.21.cloned.1.call-update) | async-done | bytes 2097168 | tf_op jit(solution)/shard_map/reduce_scatter | solution.py:217
  577.0 74.5 %reduce-scatter.23.cloned.1.call-done = bf16[1024,1024]{1,0:T(8,128)(2,1)} async-done(((bf16[4096,1024]{1,0:T(8,128)(2,1)}), bf16[1024,1024]{1,0:T(8,128)(2,1)}) %reduce-scatter.23.cloned.1.call-update) | async-done | bytes 2097168 | tf_op jit(solution)/shard_map/reduce_scatter | solution.py:220
  652.5 21.9 %reduce-scatter.25.cloned.1.call-done = bf16[256,4]{1,0:T(8,128)(2,1)} async-done(((bf16[1024,4]{1,0:T(8,128)(2,1)}), bf16[256,4]{1,0:T(8,128)(2,1)}) %reduce-scatter.25.cloned.1.call-update) | async-done | bytes 2064
  675.4 22.4 %reduce-scatter.27.cloned.1.call-done = bf16[256,4]{1,0:T(8,128)(2,1)} async-done(((bf16[1024,4]{1,0:T(8,128)(2,1)}), bf16[256,4]{1,0:T(8,128)(2,1)}) %reduce-scatter.27.cloned.1.call-update) | async-done | bytes 2064
  698.6 22.0 %reduce-scatter.29.cloned.1.call-done = bf16[256,4]{1,0:T(8,128)(2,1)} async-done(((bf16[1024,4]{1,0:T(8,128)(2,1)}), bf16[256,4]{1,0:T(8,128)(2,1)}) %reduce-scatter.29.cloned.1.call-update) | async-done | bytes 2064
  721.6 60.2 %reduce-scatter.17.cloned.1.call-done = bf16[256,3072]{1,0:T(8,128)(2,1)} async-done(((bf16[1024,3072]{1,0:T(8,128)(2,1)}), bf16[256,3072]{1,0:T(8,128)(2,1)}) %reduce-scatter.17.cloned.1.call-update) | async-done | bytes 1572880 | tf_op jit(solution)/shard_map/reduce_scatter | solution.py:211
  781.8 487.4 %all-reduce.3 = (f32[256,3072]{1,0:T(8,128)}, f32[256,1024]{1,0:T(8,128)}, f32[256,4096]{1,0:T(8,128)}, f32[1024,1024]{1,0:T(8,128)}, f32[4,256]{1,0:T(4,128)}, ...) all-reduce(bf16[256,3072]{1,0:T(8,128)(2,1)} %reduce-scatter.17.clo, ...), channel_id=1, replica_groups=mesh['ctx'=8,'wt'=4] {'ctx'}, use_global_device_ids=true, to_apply=%region_21.22 | all-reduce | flops 3149824 | bytes 18900992 | tf_op jit(solution)/shard_map/psum | solution.py:236
  (235 shorter events, 58.4 us)
Async XLA Ops:
  7.2 51.6 %all-gather.6.cloned.1.call-start = ((), (), s32[]{:S(2)}) async-start(), calls=%async_computation.8 | async-start | bytes 7864320 | tf_op jit(solution)/shard_map/all_gather | solution.py:67
  7.9 129.4 %all-gather.8.cloned.1.call-start = ((), (), s32[]{:S(2)}) async-start(), calls=%async_computation.9 | async-start | bytes 4718592 | tf_op jit(solution)/shard_map/all_gather | solution.py:87
  26.1 32.6 %copy-start.23 = (f32[128]{0:T(128)}, f32[128]{0:T(128)S(1)}, u32[]{:S(2)}) copy-start(f32[128]{0:T(128)S(1)} %broadcast_multiply_fusion.3) | copy-start | bytes 1540
  27.3 31.5 %copy-start.46 = (f32[128]{0:T(128)}, f32[128]{0:T(128)S(1)}, u32[]{:S(2)}) copy-start(f32[128]{0:T(128)S(1)} %fusion.42) | copy-start | bytes 1540
  27.3 31.4 %copy-start.25 = (f32[128]{0:T(128)}, f32[128]{0:T(128)S(1)}, u32[]{:S(2)}) copy-start(f32[128]{0:T(128)S(1)} %fusion.67) | copy-start | bytes 1540
  62.7 8.8 copy-start.44
  63.7 96.0 %all-gather.10.cloned.1.call-start = ((), (), s32[]{:S(2)}) async-start(), calls=%async_computation.10 | async-start | bytes 2621440 | tf_op jit(solution)/shard_map/all_gather | solution.py:68
  64.5 155.0 %all-gather.12.cloned.1.call-start = ((), (), s32[]{:S(2)}) async-start(), calls=%async_computation.11 | async-start | bytes 10485760 | tf_op jit(solution)/shard_map/all_gather | solution.py:69
  65.1 214.2 %all-gather.14.cloned.1.call-start = ((), (), s32[]{:S(2)}) async-start(), calls=%async_computation.12 | async-start | bytes 10485760 | tf_op jit(solution)/shard_map/all_gather | solution.py:70
  65.6 403.2 %reduce-scatter.15.cloned.1.call-start = ((), (), s32[]{:S(2)}) async-start(), calls=%async_computation.13 | async-start | bytes 9437184 | tf_op jit(solution)/shard_map/reduce_scatter | solution.py:196
  72.4 76.9 %copy-start.12 = (bf16[1,128,1024]{1,2,0:T(8,128)(2,1)}, bf16[1,128,1024]{1,2,0:T(8,128)(2,1)S(1)}, u32[]{:S(2)}) copy-start(bf16[1,128,1024]{1,2,0:T(8,128)(2,1)S(1)} %copy.36) | copy-start | bytes 786436
  154.5 8.1 copy-start.1
  279.2 8.5 slice-start.2
  279.2 6.0 copy-start.10
  279.2 6.0 copy-start.21
  279.2 6.8 copy-start.32
  279.2 8.5 slice-start.3
  287.1 5.4 slice-start
  302.5 4.8 copy-start.15
  302.6 4.8 copy-start.22
  307.3 5.8 copy-start.13
  319.2 183.4 %reduce-scatter.19.cloned.1.call-start = ((), (), s32[]{:S(2)}) async-start(), calls=%async_computation.15 | async-start | bytes 2621440 | tf_op jit(solution)/shard_map/reduce_scatter | solution.py:214
  322.2 254.8 %reduce-scatter.21.cloned.1.call-start = ((), (), s32[]{:S(2)}) async-start(), calls=%async_computation.16 | async-start | bytes 10485760 | tf_op jit(solution)/shard_map/reduce_scatter | solution.py:217
  329.3 322.2 %reduce-scatter.23.cloned.1.call-start = ((), (), s32[]{:S(2)}) async-start(), calls=%async_computation.17 | async-start | bytes 10485760 | tf_op jit(solution)/shard_map/reduce_scatter | solution.py:220
  337.5 337.0 %reduce-scatter.25.cloned.1.call-start = ((), (), s32[]{:S(2)}) async-start(), calls=%async_computation.18 | async-start | bytes 327680
  338.6 131.5 %copy-start.24 = (f32[128]{0:T(128)S(1)}, f32[128]{0:T(128)}, u32[]{:S(2)}) copy-start(f32[128]{0:T(128)} %copy-done.23) | copy-start | bytes 1540
  470.1 5.1 copy-start.47
  470.1 5.2 copy-start.26
  476.7 221.0 %reduce-scatter.27.cloned.1.call-start = ((), (), s32[]{:S(2)}) async-start(), calls=%async_computation.19 | async-start | bytes 327680
  477.7 243.0 %reduce-scatter.29.cloned.1.call-start = ((), (), s32[]{:S(2)}) async-start(), calls=%async_computation.20 | async-start | bytes 327680
  478.7 303.1 %reduce-scatter.17.cloned.1.call-start = ((), (), s32[]{:S(2)}) async-start(), calls=%async_computation.14 | async-start | bytes 7864320 | tf_op jit(solution)/shard_map/reduce_scatter | solution.py:211
  483.3 168.2 %copy-start.8 = (f32[1,128,1024]{2,1,0:T(8,128)S(1)}, f32[1,128,1024]{2,1,0:T(8,128)}, u32[]{:S(2)}) copy-start(f32[1,128,1024]{2,1,0:T(8,128)} %copy-done.7) | copy-start | bytes 1572868
  (38 other events, 90.9 us)
Sparse Core Ops, SparseCore 0:
  9.6 49.1 all-gather.5
  63.9 73.4 all-gather.7
  138.9 20.8 all-gather.9
  161.2 58.2 all-gather.11
  220.9 58.2 all-gather.13
  319.3 149.4 reduce-scatter.14
  472.1 30.4 reduce-scatter.18
  505.2 71.7 reduce-scatter.20
  579.7 71.7 reduce-scatter.22
  654.4 20.0 reduce-scatter.24
  677.6 20.0 reduce-scatter.26
  700.6 20.0 reduce-scatter.28
  723.4 58.3 reduce-scatter.16
where the time goes:
time: 1280 us
  waiting for transfers between devices  618 us (48%)
  blocking collectives  517 us (40%)
  matrix products  74.1 us (6%)
  local copies, waits for them, and re-layouts  28.4 us (2%)
  other arithmetic  22.6 us (2%)
  between operations  15.6 us (1%)
    psum x1, blocking collectives, per_device(): lax.psum((owned[0], owned[1], owned[2], owned[3], owned[4], owned[5], own...  487 us
    reduce_scatter x1, waiting for transfers between devices, per_device(): lax.psum_scatter(terms, 'ctx', scatter_dimension=0, tiled=True)  126 us
    reduce_scatter x1, waiting for transfers between devices, per_device(): lax.psum_scatter(g_down.astype(jnp.bfloat16), 'wt', scatter_dimension=0,...  74.5 us
    reduce_scatter x1, waiting for transfers between devices, per_device(): lax.psum_scatter(g_up.astype(jnp.bfloat16), 'wt', scatter_dimension=0, ti...  74.4 us
    unnamed x16, waiting for transfers between devices  68.9 us
    all_gather x1, waiting for transfers between devices, per_device(): kv_all = lax.all_gather(kv_local, 'ctx', axis=1, tiled=True)  64.9 us
    reduce_scatter x1, waiting for transfers between devices, per_device(): lax.psum_scatter(g_qkv.astype(jnp.bfloat16), 'wt', scatter_dimension=0, t...  60.2 us
    all_gather x1, waiting for transfers between devices, per_device(): lax.all_gather(w_up, 'wt', axis=0, tiled=True)  54 us
  transfers between devices with their start and end apart: 13, of which 13 were waited for; matrix products, arithmetic and copies ran while one was open for 6% of the time, Pallas kernels for 0%

commit v1 on v0

--- a/solution.py
+++ b/solution.py
@@ -9,6 +9,30 @@
 PIECE = 64
 epsilon = 1e-05
 relax = 32.0
+
+
+def register_the_ends(local):
+    passed, parts_out, h_now = (jax.lax.axis_size("wt"), jax.lax.axis_index("wt"), local.shape[0])
+    line_up = [it * passed if u == 0 else it for u, it in enumerate(local.shape)]
+    current_arr = lax.dynamic_update_slice_in_dim(
+        jnp.zeros(line_up, local.dtype), local, parts_out * h_now, axis=0
+    )
+    big = piece_next = local
+    dev_i = 1
+    while dev_i < passed // 2 + 1:
+        big = jax.lax.ppermute(big, "wt", [(u, (u + 1) % passed) for u in range(passed)])
+        current_arr = lax.dynamic_update_slice_in_dim(
+            current_arr, big, (parts_out - dev_i) % passed * h_now, axis=0
+        )
+        if 2 * dev_i < passed:
+            piece_next = jax.lax.ppermute(
+                piece_next, "wt", [(u, (u - 1) % passed) for u in range(passed)]
+            )
+            current_arr = lax.dynamic_update_slice_in_dim(
+                current_arr, piece_next, (parts_out + dev_i) % passed * h_now, axis=0
+            )
+        dev_i += 1
+    return current_arr
 
 
 def layer_norm(value, gain, shift):
@@ -66,7 +90,7 @@
     full_qkv, full_out, full_up, full_down, gains, shifts, biases, up_shift = (
         lax.all_gather(w_qkv, "wt", axis=0, tiled=True),
         lax.all_gather(w_out, "wt", axis=0, tiled=True),
-        lax.all_gather(w_up, "wt", axis=0, tiled=True),
+        register_the_ends(w_up),
         lax.all_gather(w_down, "wt", axis=0, tiled=True),
         lax.all_gather(norm_gain, "wt", axis=1, tiled=True),
         lax.all_gather(norm_shift, "wt", axis=1, tiled=True),

time: 1280 us -> 1230 us (0.961)
  waiting for transfers between devices: 618 us -> 499 us
  blocking collectives: 517 us -> 559 us
  local copies, waits for them, and re-layouts: 28.4 us -> 42.1 us
    all_gather x1, waiting for transfers between devices: 64.9 us -> 0.02 us  [per_device(): kv_all = lax.all_gather(kv_local, 'ctx', axis=1, tiled=True)]
    all_gather x1 -> x0, waiting for transfers between devices: 54 us -> none  [per_device(): lax.all_gather(w_up, 'wt', axis=0, tiled=True)]
    all_gather x1, blocking collectives: 5.16 us -> 47.1 us  [per_device(): lax.all_gather(up_bias, 'wt', axis=0, tiled=True)]
    ppermute x0 -> x3, waiting for transfers between devices: none -> 13.2 us  [the longest x2 13.2 us: register_the_ends(): jax.lax.ppermute(big, 'wt', [(u, (u + 1) % passed) for u in range(passed)])]
    unnamed x16 -> x15, waiting for transfers between devices: 68.9 us -> 68.4 us
  transfers between devices with their start and end apart: 13 -> 15, of which waited for: 13 -> 11; matrix products, arithmetic and copies ran while one was open for 6% -> 7% of each run, Pallas kernels for 0% -> 0%
where the time goes in v1:
time: 1230 us; the launch traced here: 1220 us
  blocking collectives  559 us (45%)
  waiting for transfers between devices  499 us (41%)
  matrix products  79.6 us (6%)
  local copies, waits for them, and re-layouts  42.1 us (3%)
  other arithmetic  22 us (2%)
  between operations  15.9 us (1%)
    psum x1, blocking collectives, per_device(): lax.psum((owned[0], owned[1], owned[2], owned[3], owned[4], owned[5], own...  487 us
    reduce_scatter x1, waiting for transfers between devices, per_device(): lax.psum_scatter(terms, 'ctx', scatter_dimension=0, tiled=True)  126 us
    reduce_scatter x1, waiting for transfers between devices, per_device(): lax.psum_scatter(g_down.astype(jnp.bfloat16), 'wt', scatter_dimension=0,...  74.6 us
    reduce_scatter x1, waiting for transfers between devices, per_device(): lax.psum_scatter(g_up.astype(jnp.bfloat16), 'wt', scatter_dimension=0, ti...  74.3 us
    unnamed x15, waiting for transfers between devices  68.4 us
    reduce_scatter x1, waiting for transfers between devices, per_device(): lax.psum_scatter(g_qkv.astype(jnp.bfloat16), 'wt', scatter_dimension=0, t...  60 us
    all_gather x1, blocking collectives, per_device(): lax.all_gather(up_bias, 'wt', axis=0, tiled=True)  47.1 us
    all_gather x1, waiting for transfers between devices, per_device(): lax.all_gather(w_down, 'wt', axis=0, tiled=True)  42.7 us
  transfers between devices with their start and end apart: 15, of which 11 were waited for; matrix products, arithmetic and copies ran while one was open for 7% of the time, Pallas kernels for 0%

profile of v1, /device:TPU:0, one launch (start us, length us, event | category | flops | bytes accessed | tf_op | source)
XLA Modules:
  0.0 1220.1 jit_solution(1808635301768154392)
XLA Ops:
  8.0 6.3 all_gather.27
  14.2 5.5 all_gather.25
  19.7 5.3 all_gather.24
  29.1 29.6 %all-gather.5.cloned.1.call-done = bf16[1024,3072]{1,0:T(8,128)(2,1)} async-done(((bf16[256,3072]{1,0:T(8,128)(2,1)}), bf16[1024,3072]{1,0:T(8,128)(2,1)}) %all-gather.5.cloned.1.call-update) | async-done | bytes 6291472 | tf_op jit(solution)/shard_map/all_gather | solution.py:91
  58.7 4.0 convolution_bitcast_fusion
  66.9 47.1 %all_gather.30 = bf16[4096]{0:T(1024)(128)(2,1)S(1)} all-gather(bf16[1024]{0:T(1024)(128)(2,1)S(1)} %copy-done.48), channel_id=1, replica_groups=mesh['ctx'=8,'wt'=4] {'wt'}, dimensions={0}, use_global_device_ids=true | all-gather | bytes 10240 | tf_op jit(solution)/shard_map/all_gather | solution.py:98
  115.7 4.3 broadcast_in_dim.123
  127.7 13.2 %collective-permute-done.2 = bf16[256,4096]{1,0:T(8,128)(2,1)S(1)} collective-permute-done((bf16[256,4096]{1,0:T(8,128)(2,1)}, bf16[256,4096]{1,0:T(8,128)(2,1)S(1)}, u32[]{:S(2)}, u32[]{:S(2)}) %collective-permute-start.2) | collective-permute-done | bytes 2097184 | tf_op jit(solution)/shard_map/ppermute | solution.py:23
  142.6 5.0 fusion.90
  150.9 3.9 copy.38
  169.2 7.6 convolution_add_fusion
  176.8 42.7 %all-gather.11.cloned.1.call-done = bf16[4096,1024]{1,0:T(8,128)(2,1)} async-done(((bf16[1024,1024]{1,0:T(8,128)(2,1)}), bf16[4096,1024]{1,0:T(8,128)(2,1)}) %all-gather.11.cloned.1.call-update) | async-done | bytes 8388624 | tf_op jit(solution)/shard_map/all_gather | solution.py:94
  219.5 5.8 fusion.96
  228.1 4.7 fusion.98
  232.9 7.3 fusion.47
  246.7 4.7 fusion.4
  251.4 5.8 multiply_convert_fusion
  259.2 4.1 pad_maximum_fusion
  266.3 7.0 convolution_convert_fusion.1
  274.2 7.2 convolution_convert_fusion
  286.7 126.2 %reduce-scatter.15.cloned.1.call-done = f32[128,1,2048]{0,2,1:T(8,128)} async-done(((f32[1024,1,2048]{0,2,1:T(8,128)}), f32[128,1,2048]{0,2,1:T(8,128)}) %reduce-scatter.15.cloned.1.call-update) | async-done | bytes 1048592 | tf_op jit(solution)/shard_map/reduce_scatter | solution.py:220
  414.2 5.1 fusion.43
  422.8 4.6 convolution_convert_fusion.2
  429.3 7.3 all-reduce
  436.7 9.9 reduce-scatter.19.cloned.1.call-done
  446.5 74.3 %reduce-scatter.21.cloned.1.call-done = bf16[256,4096]{1,0:T(8,128)(2,1)} async-done(((bf16[1024,4096]{1,0:T(8,128)(2,1)}), bf16[256,4096]{1,0:T(8,128)(2,1)}) %reduce-scatter.21.cloned.1.call-update) | async-done | bytes 2097168 | tf_op jit(solution)/shard_map/reduce_scatter | solution.py:241
  520.9 74.6 %reduce-scatter.23.cloned.1.call-done = bf16[1024,1024]{1,0:T(8,128)(2,1)} async-done(((bf16[4096,1024]{1,0:T(8,128)(2,1)}), bf16[1024,1024]{1,0:T(8,128)(2,1)}) %reduce-scatter.23.cloned.1.call-update) | async-done | bytes 2097168 | tf_op jit(solution)/shard_map/reduce_scatter | solution.py:244
  596.5 22.0 %reduce-scatter.25.cloned.1.call-done = bf16[256,4]{1,0:T(8,128)(2,1)} async-done(((bf16[1024,4]{1,0:T(8,128)(2,1)}), bf16[256,4]{1,0:T(8,128)(2,1)}) %reduce-scatter.25.cloned.1.call-update) | async-done | bytes 2064
  619.4 22.2 %reduce-scatter.27.cloned.1.call-done = bf16[256,4]{1,0:T(8,128)(2,1)} async-done(((bf16[1024,4]{1,0:T(8,128)(2,1)}), bf16[256,4]{1,0:T(8,128)(2,1)}) %reduce-scatter.27.cloned.1.call-update) | async-done | bytes 2064
  642.5 22.2 %reduce-scatter.29.cloned.1.call-done = bf16[256,4]{1,0:T(8,128)(2,1)} async-done(((bf16[1024,4]{1,0:T(8,128)(2,1)}), bf16[256,4]{1,0:T(8,128)(2,1)}) %reduce-scatter.29.cloned.1.call-update) | async-done | bytes 2064
  665.6 60.0 %reduce-scatter.17.cloned.1.call-done = bf16[256,3072]{1,0:T(8,128)(2,1)} async-done(((bf16[1024,3072]{1,0:T(8,128)(2,1)}), bf16[256,3072]{1,0:T(8,128)(2,1)}) %reduce-scatter.17.cloned.1.call-update) | async-done | bytes 1572880 | tf_op jit(solution)/shard_map/reduce_scatter | solution.py:235
  725.6 487.4 %all-reduce.3 = (f32[256,3072]{1,0:T(8,128)}, f32[256,1024]{1,0:T(8,128)}, f32[256,4096]{1,0:T(8,128)}, f32[1024,1024]{1,0:T(8,128)}, f32[4,256]{1,0:T(4,128)}, ...) all-reduce(bf16[256,3072]{1,0:T(8,128)(2,1)} %reduce-scatter.17.clo, ...), channel_id=1, replica_groups=mesh['ctx'=8,'wt'=4] {'ctx'}, use_global_device_ids=true, to_apply=%region_21.22 | all-reduce | flops 3149824 | bytes 18900992 | tf_op jit(solution)/shard_map/psum | solution.py:260
  (244 shorter events, 67.6 us)
Async XLA Ops:
  7.2 51.6 %all-gather.5.cloned.1.call-start = ((), (), s32[]{:S(2)}) async-start(), calls=%async_computation.8 | async-start | bytes 7864320 | tf_op jit(solution)/shard_map/all_gather | solution.py:91
  7.9 134.7 %all-gather.7.cloned.1.call-start = ((), (), s32[]{:S(2)}) async-start(), calls=%async_computation.9 | async-start | bytes 4718592 | tf_op jit(solution)/shard_map/all_gather | solution.py:111
  26.1 32.6 %copy-start.25 = (f32[128]{0:T(128)}, f32[128]{0:T(128)S(1)}, u32[]{:S(2)}) copy-start(f32[128]{0:T(128)S(1)} %broadcast_multiply_fusion.3) | copy-start | bytes 1540
  27.3 31.4 %copy-start.27 = (f32[128]{0:T(128)}, f32[128]{0:T(128)S(1)}, u32[]{:S(2)}) copy-start(f32[128]{0:T(128)S(1)} %fusion.67) | copy-start | bytes 1540
  62.7 51.9 %copy-start.47 = (s32[8,2]{0,1:T(2,128)S(1)}, s32[8,2]{0,1:T(2,128)}, u32[]{:S(2)}) copy-start(s32[8,2]{0,1:T(2,128)} %param.13) | copy-start | bytes 196
  63.8 100.1 %all-gather.9.cloned.1.call-start = ((), (), s32[]{:S(2)}) async-start(), calls=%async_computation.10 | async-start | bytes 2621440 | tf_op jit(solution)/shard_map/all_gather | solution.py:92
  64.5 155.0 %all-gather.11.cloned.1.call-start = ((), (), s32[]{:S(2)}) async-start(), calls=%async_computation.11 | async-start | bytes 10485760 | tf_op jit(solution)/shard_map/all_gather | solution.py:94
  65.1 347.8 %reduce-scatter.15.cloned.1.call-start = ((), (), s32[]{:S(2)}) async-start(), calls=%async_computation.12 | async-start | bytes 9437184 | tf_op jit(solution)/shard_map/reduce_scatter | solution.py:220
  65.1 50.1 %collective-permute-start = (bf16[256,4096]{1,0:T(8,128)(2,1)S(1)}, bf16[256,4096]{1,0:T(8,128)(2,1)}, u32[]{:S(2)}, u32[]{:S(2)}) collective-permute-start(bf16[256,4096]{1,0:T(8,128)(2,1)S(1)} %copy-done.14), channel_id=1, source_target_pairs={{0,1},{1,2},{2,3},{3,0},{4,5},{5,6},{6,7},{7,4},{8,9},{9,10},{10,1... | collective-permute-start | bytes 6291464 | tf_op jit(solution)/shard_map/ppermute | solution.py:23
  65.4 59.2 %collective-permute-start.1 = (bf16[256,4096]{1,0:T(8,128)(2,1)S(1)}, bf16[256,4096]{1,0:T(8,128)(2,1)}, u32[]{:S(2)}, u32[]{:S(2)}) collective-permute-start(bf16[256,4096]{1,0:T(8,128)(2,1)S(1)} %copy-done.14), channel_id=1, source_target_pairs={{0,3},{1,0},{2,1},{3,2},{4,7},{5,4},{6,5},{7,6},{8,11},{9,8},{10,9... | collective-permute-start | bytes 6291464 | tf_op jit(solution)/shard_map/ppermute | solution.py:28
  115.3 25.7 %collective-permute-start.2 = (bf16[256,4096]{1,0:T(8,128)(2,1)}, bf16[256,4096]{1,0:T(8,128)(2,1)S(1)}, u32[]{:S(2)}, u32[]{:S(2)}) collective-permute-start(bf16[256,4096]{1,0:T(8,128)(2,1)} %collective-permute-done), channel_id=1, source_target_pairs={{0,1},{1,2},{2,3},{3,0},{4,5},{5,6},{6,7},{7,4},{8,9},{9,10},{10,1... | collective-permute-start | bytes 6291464 | tf_op jit(solution)/shard_map/ppermute | solution.py:23
  142.6 12.3 %copy-start.12 = (bf16[1,128,1024]{1,2,0:T(8,128)(2,1)}, bf16[1,128,1024]{1,2,0:T(8,128)(2,1)S(1)}, u32[]{:S(2)}) copy-start(bf16[1,128,1024]{1,2,0:T(8,128)(2,1)S(1)} %copy.36) | copy-start | bytes 786436
  160.0 6.8 copy-start.1
  219.5 8.6 slice-start
  219.5 6.0 copy-start.22
  219.5 6.8 copy-start.35
  219.5 8.6 slice-start.1
  232.8 7.4 copy-start.9
  232.8 7.4 copy-start.54
  232.8 7.7 copy-start.21
  232.8 7.7 copy-start.41
  232.8 7.7 copy-start.46
  232.8 8.5 copy-start.52
  263.3 183.2 %reduce-scatter.19.cloned.1.call-start = ((), (), s32[]{:S(2)}) async-start(), calls=%async_computation.14 | async-start | bytes 2621440 | tf_op jit(solution)/shard_map/reduce_scatter | solution.py:238
  266.3 254.6 %reduce-scatter.21.cloned.1.call-start = ((), (), s32[]{:S(2)}) async-start(), calls=%async_computation.15 | async-start | bytes 10485760 | tf_op jit(solution)/shard_map/reduce_scatter | solution.py:241
  273.3 322.1 %reduce-scatter.23.cloned.1.call-start = ((), (), s32[]{:S(2)}) async-start(), calls=%async_computation.16 | async-start | bytes 10485760 | tf_op jit(solution)/shard_map/reduce_scatter | solution.py:244
  281.5 337.0 %reduce-scatter.25.cloned.1.call-start = ((), (), s32[]{:S(2)}) async-start(), calls=%async_computation.17 | async-start | bytes 327680
  282.7 131.5 %copy-start.26 = (f32[128]{0:T(128)S(1)}, f32[128]{0:T(128)}, u32[]{:S(2)}) copy-start(f32[128]{0:T(128)} %copy-done.25) | copy-start | bytes 1540
  420.8 220.8 %reduce-scatter.27.cloned.1.call-start = ((), (), s32[]{:S(2)}) async-start(), calls=%async_computation.18 | async-start | bytes 327680
  421.8 242.9 %reduce-scatter.29.cloned.1.call-start = ((), (), s32[]{:S(2)}) async-start(), calls=%async_computation.19 | async-start | bytes 327680
  422.8 302.9 %reduce-scatter.17.cloned.1.call-start = ((), (), s32[]{:S(2)}) async-start(), calls=%async_computation.13 | async-start | bytes 7864320 | tf_op jit(solution)/shard_map/reduce_scatter | solution.py:235
  427.4 168.0 %copy-start.8 = (f32[1,128,1024]{2,1,0:T(8,128)S(1)}, f32[1,128,1024]{2,1,0:T(8,128)}, u32[]{:S(2)}) copy-start(f32[1,128,1024]{2,1,0:T(8,128)} %copy-done.7) | copy-start | bytes 1572868
  (41 other events, 103.5 us)
Sparse Core Ops, SparseCore 0:
  9.6 49.1 all-gather.4
  63.9 73.3 all-gather.6
  138.9 20.8 all-gather.8
  161.2 58.2 all-gather.10
  263.4 149.4 reduce-scatter.14
  416.0 30.4 reduce-scatter.18
  449.1 71.7 reduce-scatter.20
  523.6 71.7 reduce-scatter.22
  598.5 19.9 reduce-scatter.24
  621.5 19.9 reduce-scatter.26
  644.6 20.0 reduce-scatter.28
  667.2 58.3 reduce-scatter.16
